TPU v7x, 32 devices: a whole 2x2x4 slice. The times are simulated.
32 devices in a mesh: chan: 8 (over z, x), tm: 4 (over y, core).
Axes of the slice: x: 2, y: 2, z: 4, core: 2. Of those that a mesh axis runs over, the one named last changes fastest.
Arguments:
- raw_traces: bfloat16 [512, 16, 4096], P('chan', 'tm'), may hold values from -6 to 6
- owner_lists: int32 [8, 128], replicated, may hold values from -1 to 511, as said below
- source_owner: int32 [2], replicated, may hold values from 0 to 7
- source_slot: int32 [2, 8], replicated, may hold values from 0 to 31, as said below
Outputs:
- correlations: float32 [1024, 16, 256], P(('chan', 'tm'))
Inputs may be any that keep to these rules, and one draw needn't show every extreme that they name: `owner_lists`: row o lists the channels owned by owner o, live entries first and then -1; each of the 512 channels appears exactly once. A quarter of the rows hold 128 live entries, half of them 3 * 16 and a quarter 64 / 2. At most 16 live entries of one row lie in one block of 64 consecutive channels, and some row has exactly 16 in some block. `source_slot`: the 8 entries of a step are distinct and below 32, so they name live channels of that owner.
All inputs are finite; a program needn't handle non-finite values.
Results may differ from a plain program's by a relative error of at most 0.0046.
Values may be sent and summed in bfloat16 or wider, within the bound.
A program may use at most 64 MiB of HBM per device.

v0:
```python
import math
import jax
import jax.numpy as jnp
from jax import lax
from jax.sharding import PartitionSpec as P

L1 = 64
L2 = 64
L = 4096
HW = 64
LAGS = 256
STEPS = 2
EPSILON = 1e-06
TWO_PI = 2.0 * math.pi


def spread(value, axis, source):
    kept = jnp.where(lax.axis_index(axis) == source, value, 0).astype(value.dtype)
    return lax.psum(kept, axis)


def make_tables():
    sample = jnp.arange(L, dtype=jnp.int32)
    window_taper = 0.5 - 0.5 * jnp.cos(TWO_PI / L * (sample.astype(jnp.float32) + 0.5))
    inner_index = jnp.arange(L2, dtype=jnp.int32)
    first_angle = (
        TWO_PI / L2 * (inner_index[:, None] * inner_index[None, :] % L2).astype(jnp.float32)
    )
    first_table = jnp.concatenate([jnp.cos(first_angle), -jnp.sin(first_angle)], axis=1).astype(
        jnp.bfloat16
    )
    outer_index = jnp.arange(L1, dtype=jnp.int32)
    twist_angle = TWO_PI / L * (outer_index[:, None] * inner_index[None, :] % L).astype(jnp.float32)
    twist_cos = jnp.cos(twist_angle)
    twist_sin = jnp.sin(twist_angle)
    half_index = jnp.arange(L1 // 2, dtype=jnp.int32)
    second_angle = (
        TWO_PI / L1 * (outer_index[:, None] * half_index[None, :] % L1).astype(jnp.float32)
    )
    second_cos = jnp.cos(second_angle)
    second_sin = jnp.sin(second_angle)
    second_table = jnp.concatenate(
        [
            jnp.concatenate([second_cos, -second_sin], axis=1),
            jnp.concatenate([second_sin, second_cos], axis=1),
        ],
        axis=0,
    )
    span_bins = 2 * HW
    band_rows = jnp.arange(3 * span_bins, dtype=jnp.int32)
    band_cols = jnp.arange(span_bins, dtype=jnp.int32)
    band = (jnp.abs(band_rows[:, None] - span_bins - band_cols[None, :]) <= HW).astype(jnp.bfloat16)
    bin_index = jnp.arange(L // 2, dtype=jnp.int32)
    counts = (jnp.minimum(bin_index, HW) + jnp.minimum(L // 2 - 1 - bin_index, HW) + 1).astype(
        jnp.float32
    )
    lag_index = jnp.arange(LAGS, dtype=jnp.int32) - LAGS // 2
    lag_angle = TWO_PI / L * (bin_index[:, None] * lag_index[None, :] % L).astype(jnp.float32)
    weights = jnp.where(bin_index == 0, 1.0, 2.0).astype(jnp.float32)[:, None]
    inverse_table = jnp.concatenate(
        [weights * jnp.cos(lag_angle), -weights * jnp.sin(lag_angle)], axis=0
    )
    return (
        window_taper,
        first_table,
        twist_cos,
        twist_sin,
        second_table,
        band,
        counts,
        inverse_table,
    )


def whiten_block(row_block, tables):
    window_taper, first_table, twist_cos, twist_sin, second_table, band, counts = tables
    row_total = row_block.shape[0]
    half_bins = L // 2
    tapered = (
        (row_block.astype(jnp.float32) * window_taper)
        .astype(jnp.bfloat16)
        .reshape(row_total, L2, L1)
    )
    section_one = jnp.einsum(
        "nab,ak->nbk", tapered, first_table, preferred_element_type=jnp.float32
    )
    real_in = section_one[:, :, :L2]
    imag_in = section_one[:, :, L2:]
    turned = jnp.concatenate(
        [real_in * twist_cos + imag_in * twist_sin, imag_in * twist_cos - real_in * twist_sin],
        axis=1,
    )
    spectrum = jnp.einsum("ntk,tj->njk", turned, second_table, precision=lax.Precision.HIGHEST)
    real_part = spectrum[:, : L1 // 2].reshape(row_total, half_bins)
    imag_part = spectrum[:, L1 // 2 :].reshape(row_total, half_bins)
    magnitude = jnp.sqrt(real_part * real_part + imag_part * imag_part).astype(jnp.bfloat16)
    span_bins = 2 * HW
    blocks = magnitude.reshape(row_total, half_bins // span_bins, span_bins)
    padded = jnp.pad(blocks, ((0, 0), (1, 1), (0, 0)))
    joined = jnp.concatenate([padded[:, :-2], padded[:, 1:-1], padded[:, 2:]], axis=2)
    smooth = jnp.einsum("nbi,ij->nbj", joined, band, preferred_element_type=jnp.float32)
    smooth = smooth.reshape(row_total, half_bins) / counts
    denominator = smooth + EPSILON
    return jnp.concatenate([real_part / denominator, imag_part / denominator], axis=1).astype(
        jnp.bfloat16
    )


def whiten_rows(traces, tables):
    row_total = traces.shape[0]
    group_rows = math.gcd(row_total, 64)
    grouped = traces.reshape(row_total // group_rows, group_rows, traces.shape[1])
    whitened = lax.map(lambda row_block: whiten_block(row_block, tables), grouped)
    return whitened.reshape(row_total, traces.shape[1])


def correlate(own_rows, sources, inverse_table, norm_scale):
    count_rows = own_rows.shape[0]
    group_rows = math.gcd(count_rows, 8)
    half_bins = L // 2
    source_real = sources[:, :, :half_bins].astype(jnp.float32)
    source_imag = sources[:, :, half_bins:].astype(jnp.float32)

    def one_group(row_block):
        block_real = row_block[:, None, :, :half_bins].astype(jnp.float32)
        block_imag = row_block[:, None, :, half_bins:].astype(jnp.float32)
        cross_real = jnp.sum(
            block_real * source_real[None] + block_imag * source_imag[None], axis=2
        )
        cross_imag = jnp.sum(
            block_imag * source_real[None] - block_real * source_imag[None], axis=2
        )
        stacked = jnp.concatenate([cross_real, cross_imag], axis=2)
        return (
            jnp.einsum("nvk,kl->nvl", stacked, inverse_table, precision=lax.Precision.HIGHEST)
            * norm_scale
        )

    grouped = own_rows.reshape(
        count_rows // group_rows, group_rows, own_rows.shape[1], own_rows.shape[2]
    )
    result = lax.map(one_group, grouped)
    return result.reshape(count_rows, sources.shape[0], inverse_table.shape[1])


def send_plan(owner_lists, own_block, block_size, send_slots):
    source_block = jnp.floor_divide(owner_lists, block_size)
    matched = (owner_lists >= 0) & (source_block == own_block)
    ranking = jnp.cumsum(matched.astype(jnp.int32), axis=1) - 1
    offsets = owner_lists - own_block * block_size
    slot_ids = jnp.arange(send_slots, dtype=jnp.int32)
    chosen = matched[:, None, :] & (ranking[:, None, :] == slot_ids[None, :, None])
    send_rows = jnp.sum(jnp.where(chosen, offsets[:, None, :], 0), axis=2)
    send_live = jnp.any(chosen, axis=2)
    return (send_rows, send_live)


def receive_plan(owner_lists, own_block, block_size, send_slots):
    my_list = lax.dynamic_index_in_dim(owner_lists, own_block, 0, keepdims=False)
    living = my_list >= 0
    source_block = jnp.floor_divide(my_list, block_size)
    position = jnp.arange(my_list.shape[0], dtype=jnp.int32)
    earlier_same = (
        (source_block[:, None] == source_block[None, :])
        & (position[None, :] < position[:, None])
        & living[None, :]
    )
    earlier = jnp.sum(earlier_same.astype(jnp.int32), axis=1)
    receive_rows = jnp.where(living, source_block * send_slots + earlier, 0)
    return (receive_rows, living)


def pack_rows(values, send_rows, send_live):
    picked = jnp.take(values, send_rows.reshape(-1), axis=0)
    return jnp.where(send_live.reshape(-1)[:, None, None], picked, jnp.zeros((), values.dtype))


def place_rows(arrived, receive_rows, living):
    picked = jnp.take(arrived, receive_rows, axis=0)
    return jnp.where(living[:, None, None], picked, jnp.zeros((), arrived.dtype))


def body(raw_traces, owner_lists, source_owner, source_slot):
    block_size, window_count, length = raw_traces.shape
    owners = lax.axis_size("chan")
    time_shards = lax.axis_size("tm")
    capacity = owner_lists.shape[1]
    send_slots = (capacity + owners - 1) // owners
    own_block = lax.axis_index("chan")
    tables = make_tables()
    forward = tables[:7]
    inverse_table = tables[7]
    norm_scale = 1.0 / math.sqrt(window_count * time_shards * (length // 2))
    slot_share = capacity // time_shards
    send_rows, send_live = send_plan(owner_lists, own_block, block_size, send_slots)
    receive_rows, living = receive_plan(owner_lists, own_block, block_size, send_slots)
    outgoing = pack_rows(raw_traces, send_rows, send_live)
    arrived = lax.all_to_all(outgoing, "chan", split_axis=0, concat_axis=0, tiled=True)
    placed = place_rows(arrived, receive_rows, living)
    spectra = whiten_rows(placed.reshape(capacity * window_count, length), forward)
    spectra = spectra.reshape(capacity, window_count, length)
    pieces = []
    for step_index in range(STEPS):
        picked = jnp.take(spectra, source_slot[step_index], axis=0)
        sources = spread(picked, "chan", source_owner[step_index])

        def stack_term(first_row, row_count, sources=sources):
            return correlate(spectra, sources, inverse_table, norm_scale)

        pieces.append(
            lax.psum_scatter(
                stack_term(jnp.int32(0), slot_share * lax.axis_size("tm")),
                "tm",
                scatter_dimension=0,
                tiled=True,
            )
        )
    result = jnp.concatenate(pieces, axis=1)
    return result


def solution(mesh):
    return jax.shard_map(
        body,
        mesh=mesh,
        in_specs=(P("chan", "tm", None), P(), P(), P()),
        out_specs=P(("chan", "tm"), None, None),
        check_vma=False,
    )
```

profile of v0, /device:TPU:0, one launch (start us, length us, event | category | flops | bytes accessed | tf_op | source)
XLA Modules:
  0.0 586.0 jit_solution(15079302522156014081)
XLA Ops:
  9.1 7.5 %gather_fusion = bf16[128,4,4096]{2,1,0:T(4,128)(2,1)} fusion(bf16[64,4,4096]{2,1,0:T(4,128)(2,1)S(1)} %copy-done, s32[1024]{0:T(1024)S(1)} %pad_clamp_fusion.3), kind=kCustom, calls=%fused_computation.2 | custom fusion | bytes 8389120 | tf_op jit(solution)/shard_map/jit(_take)/gather | solution.py:174
  16.6 6.2 %select_select_fusion.1 = bf16[128,4,4096]{2,1,0:T(4,128)(2,1)} fusion(bf16[128,4,4096]{2,1,0:T(4,128)(2,1)} %gather_fusion, pred[128]{0:T(512)(128)(4,1)S(1)} %compare_and_fusion.4, pred[128]{0:T(512)(128)(4,1)S(1)} %broadcast_in_dim.142), kind=kLoop, calls=%fused_computation.94 | loop fusion | flops 4194304 | bytes 8388864 | tf_op jit(solution)/shard_map/jit(_where)/select_n | solution.py:175
  22.8 7.4 %all-to-all-start = ((bf16[128,4,4096]{2,1,0:T(4,128)(2,1)}), bf16[128,4,4096]{2,1,0:T(4,128)(2,1)}, u32[]{:S(2)}, u32[]{:S(2)}) async-start(bf16[128,4,4096]{2,1,0:T(4,128)(2,1)} %select_select_fusion.1), calls=%async_computation | async-start | bytes 8388608 | tf_op jit(solution)/shard_map/all_to_all | solution.py:198
  35.3 9.6 %cosine_multiply_fusion = (f32[2048,256]{1,0:T(8,128)}, f32[2048,256]{1,0:T(8,128)}) fusion(s32[256]{0:T(256)S(1)} %iota_add_fusion.1, f32[2048]{0:T(1024)S(1)} %get-tuple-element.347, f32[2048]{0:T(1024)S(1)} %get-tuple-element.348), kind=kLoop, calls=%fused_computation.102 | loop fusion | flops 8388608 | bytes 4211712 | tf_op jit(solution)/shard_map/mul | solution.py:61
  44.9 78.6 %all-to-all-done = bf16[128,4,4096]{2,1,0:T(4,128)(2,1)} async-done(((bf16[128,4,4096]{2,1,0:T(4,128)(2,1)}), bf16[128,4,4096]{2,1,0:T(4,128)(2,1)}, u32[]{:S(2)}, u32[]{:S(2)}) %all-to-all-start) | async-done | bytes 4194336 | tf_op jit(solution)/shard_map/all_to_all | solution.py:198
  123.5 9.7 %gather_fusion.1 = bf16[128,4,4096]{2,1,0:T(4,128)(2,1)} fusion(bf16[128,4,4096]{2,1,0:T(4,128)(2,1)} %all-to-all-done, s32[1024]{0:T(1024)S(1)} %pad_clamp_fusion.2), kind=kCustom, calls=%fused_computation.3 | custom fusion | bytes 8389120 | tf_op jit(solution)/shard_map/jit(_take)/gather | solution.py:179
  133.2 6.9 %gather.15 = bf16[8,64,4096]{2,1,0:T(8,128)(2,1)} reshape(bf16[128,4,4096]{2,1,0:T(4,128)(2,1)} %gather_fusion.1) | data formatting | bytes 8388608 | tf_op jit(solution)/shard_map/jit(_take)/gather | solution.py:179
  140.1 3.9 select_select_fusion
  144.0 111.5 %while.39 = (s32[]{:T(128)}, bf16[8,64,4096]{2,1,0:T(8,128)(2,1)}, bf16[8,64,4096]{2,1,0:T(8,128)(2,1)}, bf16[64,128]{1,0:T(8,128)(2,1)S(1)}, f32[128,64]{0,1:T(8,128)S(1)}, /*index=5*/s32[384]{0:T(512)S(1)}) while((s32[]{:T(128)}, bf16[8,64,4096]{2,1,0:T(8,128)(2,1)}, bf16[8,64,4096]{2,1,0:T(8,128)(2,1)}, ...), condition=%wide.region_5.6_spmd.clone.clone.clone, body=%wide.region_4.5_spmd.clone.clone.sunk.clone | while | flops 578314240 | bytes 28805220 | solution.py:113
  255.4 7.2 %reshape_reshape.4 = bf16[128,4,4096]{2,1,0:T(4,128)(2,1)} reshape(bf16[8,64,4096]{2,1,0:T(8,128)(2,1)} %get-tuple-element.201) | data formatting | bytes 8388608 | tf_op jit(solution)/shard_map/reshape;reshape | solution.py:201
  270.6 3.8 pad_maximum_fusion
  274.4 7.3 %reshape_reshape_reshape.4 = bf16[16,8,4,4096]{3,2,1,0:T(4,128)(2,1)} reshape(bf16[8,64,4096]{2,1,0:T(8,128)(2,1)} %get-tuple-element.201) | data formatting | bytes 8388608 | tf_op jit(solution)/shard_map/reshape;reshape;reshape | solution.py:139
  281.7 61.0 %all-reduce.4.cloned.1.call-done = (bf16[8,4,4096]{2,1,0:T(4,128)(2,1)}, bf16[8,4,4096]{2,1,0:T(4,128)(2,1)}) async-done(((bf16[8,4,4096]{2,1,0:T(4,128)(2,1)}, bf16[8,4,4096]{2,1,0:T(4,128)(2,1)}), (bf16[8,4,4096]{2,1,0:T(4,128)(2,1)}, bf16[8,4,4096]{2,1,0:T(4,128)(2,1)})) %all-reduce.4.cloned.1.call-update) | async-done | bytes 524304 | tf_op jit(solution)/shard_map/psum | solution.py:19
  344.2 98.0 %while.37 = (s32[]{:T(128)}, f32[16,8,8,256]{3,2,1,0:T(8,128)S(1)}, bf16[16,8,4,4096]{3,2,1,0:T(4,128)(2,1)}, f32[8,4,2048]{2,0,1:T(8,128)S(1)}, f32[8,4,2048]{2,0,1:T(8,128)S(1)}, /*index=5*/f32[4096,256]{1,0:T(8,128)}) while((s32[]{:T(128)}, f32[16,8,8,256]{3,2,1,0:T(8,128)S(1)}, bf16[16,8,4,4096]{3,2,1,0:T(4,128)(2,1)}, ...), condition=%wide.region_10.12_spmd.clone, body=%wide.region_7.11_spmd.sunk.clone | while | flops 809648128 | bytes 8716365 | solution.py:142
  345.9 4.4 fusion.160
  352.0 4.4 fusion.160
  358.1 4.4 fusion.160
  364.2 4.4 fusion.160
  370.3 4.4 fusion.160
  376.5 4.4 fusion.160
  382.6 4.4 fusion.160
  388.7 4.4 fusion.160
  394.8 4.4 fusion.160
  400.9 4.4 fusion.160
  407.1 4.4 fusion.160
  413.2 4.4 fusion.160
  419.3 4.4 fusion.160
  425.4 4.4 fusion.160
  431.6 4.4 fusion.160
  437.7 4.4 fusion.160
  445.7 107.7 %while.38 = (s32[]{:T(128)}, f32[16,8,8,256]{3,2,1,0:T(8,128)}, bf16[16,8,4,4096]{3,2,1,0:T(4,128)(2,1)}, f32[8,4,2048]{2,0,1:T(8,128)S(1)}, f32[8,4,2048]{2,0,1:T(8,128)S(1)}, /*index=5*/f32[4096,256]{1,0:T(8,128)}) while((s32[]{:T(128)}, f32[16,8,8,256]{3,2,1,0:T(8,128)}, bf16[16,8,4,4096]{3,2,1,0:T(4,128)(2,1)}, ...), condition=%wide.region_16.18_spmd.clone, body=%wide.region_13.17_spmd.sunk.clone | while | flops 809648128 | bytes 8716873 | solution.py:142
  447.3 5.1 fusion.163
  454.2 5.1 fusion.163
  460.9 5.1 fusion.163
  467.6 5.1 fusion.163
  474.4 5.1 fusion.163
  481.1 5.1 fusion.163
  487.8 5.1 fusion.163
  494.5 5.1 fusion.163
  501.3 5.1 fusion.163
  508.0 5.1 fusion.163
  514.7 5.1 fusion.163
  521.4 5.1 fusion.163
  528.2 5.1 fusion.163
  534.9 5.1 fusion.163
  541.6 5.1 fusion.163
  548.4 5.1 fusion.163
  553.5 24.1 %reduce-scatter.5.cloned.1.call-done = f32[32,8,256]{2,1,0:T(8,128)} async-done(((f32[128,8,256]{2,1,0:T(8,128)}), f32[32,8,256]{2,1,0:T(8,128)}) %reduce-scatter.5.cloned.1.call-update) | async-done | bytes 262160 | tf_op jit(solution)/shard_map/reduce_scatter | solution.py:211
  (336 shorter events, 184.8 us)
Async XLA Ops:
  6.5 2.6 copy-start
  22.8 10.1 %copy-start.5 = (s32[2]{0:T(128)S(1)}, s32[2]{0:T(128)}, u32[]{:S(2)}) copy-start(s32[2]{0:T(128)} %param.14) | copy-start | bytes 28
  22.8 11.9 %copy-start.6 = (s32[2,8]{1,0:T(2,128)S(1)}, s32[2,8]{1,0:T(2,128)}, u32[]{:S(2)}) copy-start(s32[2,8]{1,0:T(2,128)} %param.15) | copy-start | bytes 196
  22.8 100.7 %all-to-all-start = ((bf16[128,4,4096]{2,1,0:T(4,128)(2,1)}), bf16[128,4,4096]{2,1,0:T(4,128)(2,1)}, u32[]{:S(2)}, u32[]{:S(2)}) async-start(bf16[128,4,4096]{2,1,0:T(4,128)(2,1)} %select_select_fusion.1), calls=%async_computation | async-start | bytes 8388608 | tf_op jit(solution)/shard_map/all_to_all | solution.py:198
  30.2 312.5 %all-reduce.4.cloned.1.call-start = ((), (), s32[]{:S(2)}) async-start(), calls=%async_computation.5 | async-start | bytes 1048576 | tf_op jit(solution)/shard_map/psum | solution.py:19
  154.8 1.2 copy-start.2
  168.8 1.2 copy-start.2
  182.8 1.2 copy-start.2
  196.7 1.2 copy-start.2
  210.6 1.2 copy-start.2
  224.5 1.2 copy-start.2
  238.4 1.2 copy-start.2
  252.4 1.2 copy-start.2
  262.6 8.0 %copy-start.3 = (f32[2048,256]{1,0:T(8,128)S(1)}, f32[2048,256]{1,0:T(8,128)}, u32[]{:S(2)}) copy-start(f32[2048,256]{1,0:T(8,128)} %get-tuple-element.333) | copy-start | bytes 6291460
  270.5 282.9 %reduce-scatter.3.cloned.1.call-start = ((), (), s32[]{:S(2)}) async-start(), calls=%async_computation.3 | async-start | bytes 1310720 | tf_op jit(solution)/shard_map/reduce_scatter | solution.py:211
  442.1 1.1 copy-start.4
  443.2 134.4 %reduce-scatter.5.cloned.1.call-start = ((), (), s32[]{:S(2)}) async-start(), calls=%async_computation.4 | async-start | bytes 1310720 | tf_op jit(solution)/shard_map/reduce_scatter | solution.py:211
  553.4 26.0 %copy-start.1 = (bf16[64,4,4096]{2,1,0:T(4,128)(2,1)S(1)}, bf16[64,4,4096]{2,1,0:T(4,128)(2,1)}, u32[]{:S(2)}) copy-start(bf16[64,4,4096]{2,1,0:T(4,128)(2,1)} %param.12) | copy-start | bytes 6291460
Sparse Core Ops, SparseCore 0:
  270.6 72.0 all-reduce.3
  443.3 23.9 reduce-scatter.2
  553.6 23.9 reduce-scatter.4
where the time goes:
time: 590 us; the launch traced here: 586 us
  matrix products  193 us (33%)
  waiting for transfers between devices  164 us (28%)
  local copies, waits for them, and re-layouts  119 us (20%)
  other arithmetic  87.6 us (15%)
  between operations  14.6 us (2%)
  starting transfers between devices  7.53 us (1%)
    dot_general x32, matrix products, one_group(): jnp.einsum('nvk,kl->nvl', stacked, inverse_table, precision=lax.Precision...  152 us
    all_to_all x1, waiting for transfers between devices, body(): lax.all_to_all(outgoing, 'chan', split_axis=0, concat_axis=0, tiled=True)  78.6 us
    psum x1, waiting for transfers between devices, spread(): return lax.psum(kept, axis)  61 us
    squeeze x32, local copies, waits for them, and re-layouts, correlate(): result = lax.map(one_group, grouped)  33.4 us
    reduce_scatter x2, waiting for transfers between devices, body(): lax.psum_scatter(stack_term(jnp.int32(0), slot_share * lax.axis_size('tm'...  24.1 us
    convert_element_type x16, local copies, waits for them, and re-layouts, whiten_block(): row_block.astype(jnp.float32) * window_taper  21.4 us
    dot_general x8, matrix products, whiten_block(): jnp.einsum('ntk,tj->njk', turned, second_table, precision=lax.Precision.H...  20.9 us
    reduce_sum x32, other arithmetic, one_group(): jnp.sum(block_real * source_real[None] + block_imag * source_imag[None],...  18.1 us
  transfers between devices with their start and end apart: 4, of which 3 were waited for; matrix products, arithmetic and copies ran while one was open for 23% of the time, Pallas kernels for 0%

commit v1 on v0

--- a/solution.py
+++ b/solution.py
@@ -16,7 +16,7 @@
 
 def spread(value, axis, source):
     kept = jnp.where(lax.axis_index(axis) == source, value, 0).astype(value.dtype)
-    return lax.psum(kept, axis)
+    return jnp.sum(lax.all_gather(kept, axis), axis=0)
 
 
 def make_tables():

time: 590 us -> 566 us (0.959)
  waiting for transfers between devices: 164 us -> 138 us
    psum x1 -> x0, waiting for transfers between devices: 61 us -> none  [spread(): return lax.psum(kept, axis)]
    all_gather x0 -> x2, waiting for transfers between devices: none -> 25.6 us  [spread(): return jnp.sum(lax.all_gather(kept, axis), axis=0)]
    all_to_all x1, waiting for transfers between devices: 78.6 us -> 88.8 us  [body(): lax.all_to_all(outgoing, 'chan', split_axis=0, concat_axis=0, tiled=True)]
  transfers between devices with their start and end apart: 4 -> 5, of which waited for: 3 -> 3; matrix products, arithmetic and copies ran while one was open for 23% -> 42% of each run, Pallas kernels for 0% -> 0%
where the time goes in v1:
time: 566 us; the launch traced here: 562 us
  matrix products  193 us (34%)
  waiting for transfers between devices  138 us (24%)
  local copies, waits for them, and re-layouts  118 us (21%)
  other arithmetic  88.4 us (16%)
  between operations  14.5 us (3%)
  starting transfers between devices  8.24 us (1%)
    dot_general x32, matrix products, one_group(): jnp.einsum('nvk,kl->nvl', stacked, inverse_table, precision=lax.Precision...  152 us
    all_to_all x1, waiting for transfers between devices, body(): lax.all_to_all(outgoing, 'chan', split_axis=0, concat_axis=0, tiled=True)  88.8 us
    squeeze x32, local copies, waits for them, and re-layouts, correlate(): result = lax.map(one_group, grouped)  33.4 us
    all_gather x2, waiting for transfers between devices, spread(): return jnp.sum(lax.all_gather(kept, axis), axis=0)  25.6 us
    reduce_scatter x2, waiting for transfers between devices, body(): lax.psum_scatter(stack_term(jnp.int32(0), slot_share * lax.axis_size('tm'...  23.7 us
    convert_element_type x16, local copies, waits for them, and re-layouts, whiten_block(): row_block.astype(jnp.float32) * window_taper  21.5 us
    dot_general x8, matrix products, whiten_block(): jnp.einsum('ntk,tj->njk', turned, second_table, precision=lax.Precision.H...  20.9 us
    reduce_sum x32, other arithmetic, one_group(): jnp.sum(block_real * source_real[None] + block_imag * source_imag[None],...  18.1 us
  transfers between devices with their start and end apart: 5, of which 3 were waited for; matrix products, arithmetic and copies ran while one was open for 42% of the time, Pallas kernels for 0%

profile of v1, /device:TPU:0, one launch (start us, length us, event | category | flops | bytes accessed | tf_op | source)
XLA Modules:
  0.0 561.7 jit_solution(10236998391691495366)
XLA Ops:
  9.1 7.5 %gather_fusion = bf16[128,4,4096]{2,1,0:T(4,128)(2,1)} fusion(bf16[64,4,4096]{2,1,0:T(4,128)(2,1)S(1)} %copy-done, s32[1024]{0:T(1024)S(1)} %pad_clamp_fusion.3), kind=kCustom, calls=%fused_computation.2 | custom fusion | bytes 8389120 | tf_op jit(solution)/shard_map/jit(_take)/gather | solution.py:174
  16.6 6.2 %select_select_fusion.1 = bf16[128,4,4096]{2,1,0:T(4,128)(2,1)} fusion(bf16[128,4,4096]{2,1,0:T(4,128)(2,1)} %gather_fusion, pred[128]{0:T(512)(128)(4,1)S(1)} %compare_and_fusion.4, pred[128]{0:T(512)(128)(4,1)S(1)} %broadcast_in_dim.142), kind=kLoop, calls=%fused_computation.94 | loop fusion | flops 4194304 | bytes 8388864 | tf_op jit(solution)/shard_map/jit(_where)/select_n | solution.py:175
  22.8 7.4 %all-to-all-start = ((bf16[128,4,4096]{2,1,0:T(4,128)(2,1)}), bf16[128,4,4096]{2,1,0:T(4,128)(2,1)}, u32[]{:S(2)}, u32[]{:S(2)}) async-start(bf16[128,4,4096]{2,1,0:T(4,128)(2,1)} %select_select_fusion.1), calls=%async_computation | async-start | bytes 8388608 | tf_op jit(solution)/shard_map/all_to_all | solution.py:198
  34.7 88.8 %all-to-all-done = bf16[128,4,4096]{2,1,0:T(4,128)(2,1)} async-done(((bf16[128,4,4096]{2,1,0:T(4,128)(2,1)}), bf16[128,4,4096]{2,1,0:T(4,128)(2,1)}, u32[]{:S(2)}, u32[]{:S(2)}) %all-to-all-start) | async-done | bytes 4194336 | tf_op jit(solution)/shard_map/all_to_all | solution.py:198
  123.5 9.7 %gather_fusion.1 = bf16[128,4,4096]{2,1,0:T(4,128)(2,1)} fusion(bf16[128,4,4096]{2,1,0:T(4,128)(2,1)} %all-to-all-done, s32[1024]{0:T(1024)S(1)} %pad_clamp_fusion.2), kind=kCustom, calls=%fused_computation.3 | custom fusion | bytes 8389120 | tf_op jit(solution)/shard_map/jit(_take)/gather | solution.py:179
  133.2 6.9 %gather.15 = bf16[8,64,4096]{2,1,0:T(8,128)(2,1)} reshape(bf16[128,4,4096]{2,1,0:T(4,128)(2,1)} %gather_fusion.1) | data formatting | bytes 8388608 | tf_op jit(solution)/shard_map/jit(_take)/gather | solution.py:179
  140.1 3.9 select_select_fusion
  144.0 111.6 %while.39 = (s32[]{:T(128)}, bf16[8,64,4096]{2,1,0:T(8,128)(2,1)}, bf16[8,64,4096]{2,1,0:T(8,128)(2,1)}, bf16[64,128]{1,0:T(8,128)(2,1)S(1)}, f32[128,64]{0,1:T(8,128)S(1)}, /*index=5*/s32[384]{0:T(512)S(1)}) while((s32[]{:T(128)}, bf16[8,64,4096]{2,1,0:T(8,128)(2,1)}, bf16[8,64,4096]{2,1,0:T(8,128)(2,1)}, ...), condition=%wide.region_5.6_spmd.clone.clone.clone, body=%wide.region_4.5_spmd.clone.clone.sunk.clone | while | flops 578314240 | bytes 28805220 | solution.py:113
  255.5 7.2 %reshape_reshape.4 = bf16[128,4,4096]{2,1,0:T(4,128)(2,1)} reshape(bf16[8,64,4096]{2,1,0:T(8,128)(2,1)} %get-tuple-element.201) | data formatting | bytes 8388608 | tf_op jit(solution)/shard_map/reshape;reshape | solution.py:201
  267.5 8.3 %cosine_multiply_fusion = (f32[2048,256]{1,0:T(8,128)S(1)}, f32[2048,256]{1,0:T(8,128)S(1)}) fusion(s32[256]{0:T(256)S(1)} %iota_add_fusion.1, f32[2048]{0:T(1024)S(1)} %get-tuple-element.343, f32[2048]{0:T(1024)S(1)} %get-tuple-element.344), kind=kLoop, calls=%fused_computation.102 | loop fusion | flops 8388608 | bytes 4211712 | tf_op jit(solution)/shard_map/mul | solution.py:61
  278.0 7.2 %reshape_reshape_reshape.4 = bf16[16,8,4,4096]{3,2,1,0:T(4,128)(2,1)} reshape(bf16[8,64,4096]{2,1,0:T(8,128)(2,1)} %get-tuple-element.201) | data formatting | bytes 8388608 | tf_op jit(solution)/shard_map/reshape;reshape;reshape | solution.py:139
  285.2 3.0 gather_fusion.3
  289.4 25.6 %all-gather.5.cloned.1.call-done = bf16[64,4,4096]{2,1,0:T(4,128)(2,1)} async-done(((bf16[8,4,4096]{2,1,0:T(4,128)(2,1)}), bf16[64,4,4096]{2,1,0:T(4,128)(2,1)}) %all-gather.5.cloned.1.call-update) | async-done | bytes 2097168 | tf_op jit(solution)/shard_map/all_gather | solution.py:19
  318.3 98.0 %while.37 = (s32[]{:T(128)}, f32[16,8,8,256]{3,2,1,0:T(8,128)S(1)}, bf16[16,8,4,4096]{3,2,1,0:T(4,128)(2,1)}, f32[8,4,2048]{2,0,1:T(8,128)S(1)}, f32[8,4,2048]{2,0,1:T(8,128)S(1)}, /*index=5*/f32[4096,256]{1,0:T(8,128)}) while((s32[]{:T(128)}, f32[16,8,8,256]{3,2,1,0:T(8,128)S(1)}, bf16[16,8,4,4096]{3,2,1,0:T(4,128)(2,1)}, ...), condition=%wide.region_10.12_spmd.clone, body=%wide.region_7.11_spmd.sunk.clone | while | flops 809648128 | bytes 8716365 | solution.py:142
  320.0 4.4 fusion.160
  326.1 4.4 fusion.160
  332.2 4.5 fusion.160
  338.3 4.4 fusion.160
  344.5 4.4 fusion.160
  350.6 4.5 fusion.160
  356.7 4.4 fusion.160
  362.9 4.4 fusion.160
  369.0 4.4 fusion.160
  375.1 4.4 fusion.160
  381.2 4.4 fusion.160
  387.4 4.4 fusion.160
  393.5 4.4 fusion.160
  399.6 4.4 fusion.160
  405.7 4.4 fusion.160
  411.8 4.4 fusion.160
  421.7 107.8 %while.38 = (s32[]{:T(128)}, f32[16,8,8,256]{3,2,1,0:T(8,128)}, bf16[16,8,4,4096]{3,2,1,0:T(4,128)(2,1)}, f32[8,4,2048]{2,0,1:T(8,128)S(1)}, f32[8,4,2048]{2,0,1:T(8,128)S(1)}, /*index=5*/f32[4096,256]{1,0:T(8,128)}) while((s32[]{:T(128)}, f32[16,8,8,256]{3,2,1,0:T(8,128)}, bf16[16,8,4,4096]{3,2,1,0:T(4,128)(2,1)}, ...), condition=%wide.region_16.18_spmd.clone, body=%wide.region_13.17_spmd.sunk.clone | while | flops 809648128 | bytes 8716873 | solution.py:142
  423.4 5.2 fusion.163
  430.2 5.1 fusion.163
  437.0 5.1 fusion.163
  443.7 5.1 fusion.163
  450.5 5.1 fusion.163
  457.2 5.1 fusion.163
  463.9 5.1 fusion.163
  470.6 5.1 fusion.163
  477.4 5.1 fusion.163
  484.1 5.1 fusion.163
  490.8 5.1 fusion.163
  497.6 5.1 fusion.163
  504.3 5.1 fusion.163
  511.0 5.1 fusion.163
  517.7 5.1 fusion.163
  524.5 5.1 fusion.163
  529.6 23.7 %reduce-scatter.5.cloned.1.call-done = f32[32,8,256]{2,1,0:T(8,128)} async-done(((f32[128,8,256]{2,1,0:T(8,128)}), f32[32,8,256]{2,1,0:T(8,128)}) %reduce-scatter.5.cloned.1.call-update) | async-done | bytes 262160 | tf_op jit(solution)/shard_map/reduce_scatter | solution.py:211
  (340 shorter events, 188.3 us)
Async XLA Ops:
  6.5 2.6 copy-start
  22.8 10.2 %copy-start.4 = (s32[2]{0:T(128)S(1)}, s32[2]{0:T(128)}, u32[]{:S(2)}) copy-start(s32[2]{0:T(128)} %param.14) | copy-start | bytes 28
  22.8 11.3 %copy-start.5 = (s32[2,8]{1,0:T(2,128)S(1)}, s32[2,8]{1,0:T(2,128)}, u32[]{:S(2)}) copy-start(s32[2,8]{1,0:T(2,128)} %param.15) | copy-start | bytes 196
  22.8 100.7 %all-to-all-start = ((bf16[128,4,4096]{2,1,0:T(4,128)(2,1)}), bf16[128,4,4096]{2,1,0:T(4,128)(2,1)}, u32[]{:S(2)}, u32[]{:S(2)}) async-start(bf16[128,4,4096]{2,1,0:T(4,128)(2,1)} %select_select_fusion.1), calls=%async_computation | async-start | bytes 8388608 | tf_op jit(solution)/shard_map/all_to_all | solution.py:198
  30.2 284.8 %all-gather.5.cloned.1.call-start = ((), (), s32[]{:S(2)}) async-start(), calls=%async_computation.5 | async-start | bytes 2359296 | tf_op jit(solution)/shard_map/all_gather | solution.py:19
  154.8 1.2 copy-start.2
  168.8 1.2 copy-start.2
  182.8 1.2 copy-start.2
  196.7 1.2 copy-start.2
  210.6 1.2 copy-start.2
  224.6 1.2 copy-start.2
  238.5 1.2 copy-start.2
  252.5 1.2 copy-start.2
  266.6 150.7 %all-gather.7.cloned.1.call-start = ((), (), s32[]{:S(2)}) async-start(), calls=%async_computation.6 | async-start | bytes 2359296 | tf_op jit(solution)/shard_map/all_gather | solution.py:19
  289.1 240.5 %reduce-scatter.3.cloned.1.call-start = ((), (), s32[]{:S(2)}) async-start(), calls=%async_computation.3 | async-start | bytes 1310720 | tf_op jit(solution)/shard_map/reduce_scatter | solution.py:211
  416.3 1.0 copy-start.3
  417.3 136.0 %reduce-scatter.5.cloned.1.call-start = ((), (), s32[]{:S(2)}) async-start(), calls=%async_computation.4 | async-start | bytes 1310720 | tf_op jit(solution)/shard_map/reduce_scatter | solution.py:211
  529.5 25.6 %copy-start.1 = (bf16[64,4,4096]{2,1,0:T(4,128)(2,1)S(1)}, bf16[64,4,4096]{2,1,0:T(4,128)(2,1)}, u32[]{:S(2)}) copy-start(bf16[64,4,4096]{2,1,0:T(4,128)(2,1)} %param.12) | copy-start | bytes 6291460
Sparse Core Ops, SparseCore 0:
  266.7 48.2 all-gather.4
  317.1 47.6 all-gather.6
  417.4 23.6 reduce-scatter.2
  529.7 23.5 reduce-scatter.4
